TPU v7x, 768 devices: a whole 4x8x12 slice. The times are simulated.
768 devices in a mesh: sub: 96 (over y, z), grp: 8 (over x, core).
Axes of the slice: x: 4, y: 8, z: 12, core: 2. Of those that a mesh axis runs over, the one named last changes fastest.
Arguments:
- rhs: float32 [96, 8, 64, 128], P('sub', 'grp')
- guess: float32 [96, 8, 64, 128], P('sub', 'grp'), may hold values from -6 to 6
- blocks: bfloat16 [96, 8, 64, 64, 128], P('sub', 'grp')
- valve: int32 [96, 8, 128], P('sub', 'grp'), may hold values 0 or 1
- jscale: float32 [96, 8, 64, 128], P('sub', 'grp'), may hold values from 0.1 to 0.4
- prolong: float32 [96, 8, 64, 128], P('sub', 'grp'), may hold values from -0.75 to 0.75
- agg_map: int32 [96, 8, 128], P('sub', 'grp'), may hold values from 0 to 47
- cdiag: float32 [36864], P(('sub', 'grp')), may hold values from 0.5 to 2
- coff: bfloat16 [36864, 36864], P(('sub', 'grp')), may hold values from -0.125 to 0.125
- send_rows: int32 [96, 8, 2, 128], P('sub', 'grp'), may hold values from 0 to 127
- recv_rows: int32 [96, 8, 2, 128], P('sub', 'grp'), may hold values from 0 to 127
- live_counts: int32 [96, 8, 2], P('sub', 'grp'), may hold values from 32 to 128, as said below
Outputs:
- solution: float32 [96, 8, 64, 128], P('sub', 'grp')
- next_basis: float32 [96, 8, 64, 128], P('sub', 'grp')
Inputs may be any that keep to these rules, and one draw needn't show every extreme that they name: `send_rows`: block numbers of the sending subdomain. `recv_rows`: block numbers of the receiving subdomain; several slots may name one block. `live_counts`: some subdomain has every slot live in both lists. `agg_map`: aggregates may be empty.
All inputs are finite; a program needn't handle non-finite values. No bound on the sum of `valve` on one device may be relied on, other than what follows from the above.
Results may differ from a plain program's by a relative error of at most 0.003.
Values may be sent and summed in bfloat16 or wider, within the bound.
A program may use at most 32 MiB of HBM per device.

v0:
```python
import jax
import jax.numpy as jnp
from jax import lax
from jax.sharding import PartitionSpec as P

ITERS = 2


penalty_gain = 3.0
coupling = 0.5


def extended(cells, sides, width):
    for axis, dim in sides:
        count = lax.axis_size(axis)
        ends = count - 1
        head = lax.slice_in_dim(cells, 0, width, axis=dim)
        tail = lax.slice_in_dim(cells, cells.shape[dim] - width, cells.shape[dim], axis=dim)
        cells = jnp.concatenate(
            [
                lax.ppermute(tail, axis, [(i, (i + 1) % count) for i in range(ends)]),
                cells,
                lax.ppermute(head, axis, [((i + 1) % count, i) for i in range(ends)]),
            ],
            axis=dim,
        )
    return cells


def solve_small(gram, target):
    count = target.shape[0]
    matrix = [[gram[row, col] for col in range(count)] for row in range(count)]
    vector = [target[row] for row in range(count)]
    for pivot in range(count):
        for row in range(pivot + 1, count):
            factor = matrix[row][pivot] / matrix[pivot][pivot]
            for col in range(pivot, count):
                matrix[row][col] = matrix[row][col] - factor * matrix[pivot][col]
            vector[row] = vector[row] - factor * vector[pivot]
    result = [None] * count
    for row in range(count - 1, -1, -1):
        total = vector[row]
        for col in range(row + 1, count):
            total = total - matrix[row][col] * result[col]
        result[row] = total / matrix[row][row]
    return result


def on_device(
    rhs,
    guess,
    blocks,
    valve,
    jscale,
    prolong,
    agg_map,
    cdiag,
    coff,
    send_rows,
    recv_rows,
    live_counts,
):
    highest = lax.Precision.HIGHEST
    right = rhs[0, 0]
    start_vec = guess[0, 0]
    block_mat = blocks[0, 0].astype(jnp.float32)
    scaling = jscale[0, 0]
    weights = prolong[0, 0]
    nblk = right.shape[1]
    places = jnp.arange(nblk, dtype=jnp.int32)
    slots = jnp.arange(send_rows.shape[3], dtype=jnp.int32)
    send_sel = [
        (places[:, None] == send_rows[0, 0, side][None, :]).astype(jnp.float32) for side in (0, 1)
    ]
    recv_sel = [
        (
            (recv_rows[0, 0, side][:, None] == places[None, :])
            & (slots < live_counts[0, 0, side])[:, None]
        ).astype(jnp.float32)
        for side in (0, 1)
    ]
    penalty_row = penalty_gain * valve[0, 0].astype(jnp.float32)
    coarse_count = cdiag.shape[0]
    agg_sel = (agg_map[0, 0][:, None] == jnp.arange(coarse_count, dtype=jnp.int32)[None, :]).astype(
        jnp.float32
    )

    def operate(field):
        out = (
            jnp.einsum("ijb,jb->ib", block_mat, field, precision=highest)
            + penalty_row[None, :] * field
        )
        upward = jnp.dot(field, send_sel[0], precision=highest)
        downward = jnp.dot(field, send_sel[1], precision=highest)
        stacked = jnp.stack([upward, downward])[None]
        padded = extended(stacked, (("sub", 0),), 1)
        below = padded[0, 0]
        above = padded[2, 1]
        incoming = jnp.dot(below, recv_sel[0], precision=highest) + jnp.dot(
            above, recv_sel[1], precision=highest
        )
        return out - coupling * incoming

    first = right - operate(start_vec)
    directions = []
    hess = jnp.zeros((ITERS + 1, ITERS), jnp.float32)
    beta = jnp.sqrt(lax.psum(jnp.sum(first * first), ("sub", "grp")))
    basis = [first / beta]
    for column in range(ITERS):
        precondition_field = basis[column]
        weighted = jnp.sum(weights * precondition_field, axis=0)
        precondition_coarse = jnp.dot(weighted, agg_sel, precision=highest)
        coarse_half = precondition_coarse.astype(jnp.bfloat16)
        gathered = lax.all_gather(coarse_half, ("sub", "grp"), axis=0, tiled=True)
        precondition_product = jnp.dot(coff, gathered, preferred_element_type=jnp.float32)
        coarse_sol = cdiag * precondition_coarse + precondition_product
        spread = jnp.dot(agg_sel, coarse_sol, precision=highest)
        direction = scaling * precondition_field + weights * spread[None, :]
        image = operate(direction)
        local_terms = jnp.stack(
            [jnp.sum(vector * image) for vector in basis] + [jnp.sum(image * image)]
        )
        totals = lax.psum(local_terms, ("sub", "grp"))
        extend_image = image
        extend_hess = hess
        heights = totals[: column + 1]
        energy = totals[column + 1]
        for row in range(column + 1):
            extend_image = extend_image - heights[row] * basis[row]
        remainder = energy - jnp.sum(heights * heights)
        height = jnp.sqrt(jnp.maximum(remainder, 0.01 * energy))
        extend_hess = (
            extend_hess.at[: column + 1, column].set(heights).at[column + 1, column].set(height)
        )
        heights, height, fresh, hess = (heights, height, extend_image / height, extend_hess)
        basis.append(fresh)
        directions.append(direction)
    gram = jnp.dot(hess.T, hess, precision=highest)
    coeffs = solve_small(gram, beta * hess[0])
    solution = start_vec
    for column in range(ITERS):
        solution = solution + coeffs[column] * directions[column]
    return (solution[None, None], basis[ITERS][None, None])


def solution(mesh):
    return jax.shard_map(
        on_device,
        mesh=mesh,
        in_specs=(
            P("sub", "grp", None, None),
            P("sub", "grp", None, None),
            P("sub", "grp", None, None, None),
            P("sub", "grp", None),
            P("sub", "grp", None, None),
            P("sub", "grp", None, None),
            P("sub", "grp", None),
            P(("sub", "grp")),
            P(("sub", "grp"), None),
            P("sub", "grp", None, None),
            P("sub", "grp", None, None),
            P("sub", "grp", None),
        ),
        out_specs=(P("sub", "grp", None, None), P("sub", "grp", None, None)),
        check_vma=False,
    )
```

profile of v0, /device:TPU:1, one launch (start us, length us, event | category | flops | bytes accessed | tf_op | source)
XLA Modules:
  0.0 1325.4 jit_solution(2019140828051896604)
XLA Ops:
  7.2 0.9 slice_bitcast_fusion.15
  8.1 1.1 convolution_bitcast_fusion.4
  9.2 0.9 convolution_bitcast_fusion.5
  10.8 1.3 collective-permute-start.1
  12.0 6.1 collective-permute-start
  18.1 1.3 slice_bitcast_fusion.13
  19.5 1.3 fusion.62
  20.8 1.2 iota_compare_fusion.15
  21.9 0.7 multiply_bitcast_fusion
  22.6 2.2 fusion
  24.8 0.6 iota_compare_fusion.16
  25.5 1.0 fusion.23
  26.5 2.3 multiply_reduce_fusion.5
  28.8 118.6 %psum.21 = f32[]{:T(128)} all-reduce(f32[]{:T(128)} %get-tuple-element.76), channel_id=1, replica_groups=mesh['sub'=96,'grp'=8] {'sub','grp'}, use_global_device_ids=true, to_apply=%region_1.0 | all-reduce | flops 1 | bytes 8 | tf_op jit(solution)/shard_map/psum | solution.py:107
  148.1 0.8 fusion.25
  148.9 1.4 fusion.63
  151.0 1.4 dynamic-update-slice.8
  152.5 445.4 %all-reduce.6.cloned.1.call-done = bf16[36864]{0:T(1024)(128)(2,1)} async-done(((bf16[36864]{0:T(1024)(128)(2,1)}), bf16[36864]{0:T(1024)(128)(2,1)}) %all-reduce.6.cloned.1.call-update) | async-done | bytes 73744
  597.9 1.0 reshape.176
  598.9 1.8 fusion.13
  600.7 0.9 convolution_bitcast_fusion.8
  602.0 1.3 collective-permute-start.3
  603.3 4.0 collective-permute-start.2
  607.9 0.7 collective-permute-done.2
  608.6 1.6 multiply_reduce_fusion.4
  610.2 1.9 pad_maximum_fusion
  612.0 111.5 %psum.22 = f32[2]{0:T(128)S(1)} all-reduce(f32[2]{0:T(128)} %pad_maximum_fusion), channel_id=1, replica_groups=mesh['sub'=96,'grp'=8] {'sub','grp'}, use_global_device_ids=true, to_apply=%region_5.0 | all-reduce | flops 2 | bytes 16 | tf_op jit(solution)/shard_map/psum | solution.py:123
  723.5 0.6 fusion.61
  726.8 2.1 fusion.27
  728.9 1.4 fusion.64
  730.9 1.4 dynamic-update-slice.9
  733.0 0.7 compare_reduce_fusion
  733.7 0.7 scatter.14
  734.4 442.2 %all-reduce.8.cloned.1.call-done = bf16[36864]{0:T(1024)(128)(2,1)} async-done(((bf16[36864]{0:T(1024)(128)(2,1)}), bf16[36864]{0:T(1024)(128)(2,1)}) %all-reduce.8.cloned.1.call-update) | async-done | bytes 73744
  1176.7 1.0 reshape.184
  1177.7 1.8 fusion.11
  1179.5 0.9 convolution_bitcast_fusion.6
  1180.8 1.3 collective-permute-start.5
  1182.1 4.0 collective-permute-start.4
  1186.7 0.7 collective-permute-done.4
  1187.4 1.5 multiply_reduce_fusion.2
  1188.9 1.9 pad_maximum_fusion.1
  1190.9 111.5 %psum.23 = f32[3]{0:T(128)S(1)} all-reduce(f32[3]{0:T(128)S(1)} %pad_maximum_fusion.1), channel_id=1, replica_groups=mesh['sub'=96,'grp'=8] {'sub','grp'}, use_global_device_ids=true, to_apply=%region_11.0 | all-reduce | flops 3 | bytes 24 | tf_op jit(solution)/shard_map/psum | solution.py:123
  1303.0 0.6 multiply_reduce_fusion.6
  1303.7 1.9 broadcast_select_fusion
  1305.6 1.3 scatter.16
  1309.5 0.7 fusion.57
  1315.9 2.7 fusion.32
  (73 shorter events, 6.2 us)
Async XLA Ops:
  7.2 591.7 %copy-start = (bf16[48,36864]{1,0:T(8,128)(2,1)S(1)}, bf16[48,36864]{1,0:T(8,128)(2,1)}, u32[]{:S(2)}) copy-start(bf16[48,36864]{1,0:T(8,128)(2,1)} %param.28) | copy-start | bytes 10616836
  7.2 590.7 %all-reduce.6.cloned.1.call-start = ((), (), s32[]{:S(2)}) async-start(), calls=%async_computation | async-start | bytes 147456
  10.8 14.7 %collective-permute-start.1 = (f32[1,2,64,128]{3,2,1,0:T(8,128)}, f32[1,2,64,128]{3,2,1,0:T(8,128)}, u32[]{:S(2)}, u32[]{:S(2)}) collective-permute-start(f32[1,2,64,128]{3,2,1,0:T(8,128)} %maximum_bitcast_fusion), channel_id=1, source_target_pairs={{8,0},{16,8},{24,16},{32,24},{40,32},{48,40},{56,48},{64,56},{72,6... | collective-permute-start | bytes 196616 | tf_op jit(solution)/shard_map/ppermute | solution.py:23
  12.0 14.5 %collective-permute-start = (f32[1,2,64,128]{3,2,1,0:T(8,128)}, f32[1,2,64,128]{3,2,1,0:T(8,128)}, u32[]{:S(2)}, u32[]{:S(2)}) collective-permute-start(f32[1,2,64,128]{3,2,1,0:T(8,128)} %maximum_bitcast_fusion), channel_id=1, source_target_pairs={{0,8},{8,16},{16,24},{24,32},{32,40},{40,48},{48,56},{56,64},{64,7... | collective-permute-start | bytes 196616 | tf_op jit(solution)/shard_map/ppermute | solution.py:21
  22.6 586.0 %copy-start.12 = (f32[128]{0:T(128)}, f32[128]{0:T(128)S(1)}, u32[]{:S(2)}) copy-start(f32[128]{0:T(128)S(1)} %multiply_bitcast_fusion) | copy-start | bytes 1540
  25.5 3.3 copy-start.14
  152.4 1024.2 %all-reduce.8.cloned.1.call-start = ((), (), s32[]{:S(2)}) async-start(), calls=%async_computation.1 | async-start | bytes 147456
  597.8 3.7 copy-start.3
  597.8 3.7 copy-start.7
  597.9 3.7 copy-start.10
  598.8 8.4 copy-start.1
  598.8 8.8 copy-start.17
  598.9 8.8 copy-start.19
  598.9 9.7 copy-start.15
  601.6 8.5 copy-start.5
  602.0 5.7 collective-permute-start.3
  603.3 5.3 collective-permute-start.2
  1176.7 3.7 copy-start.8
  1176.7 3.7 copy-start.9
  1176.7 3.7 copy-start.11
  1177.6 8.5 copy-start.2
  1177.7 8.8 copy-start.18
  1177.7 8.8 copy-start.20
  1177.7 9.7 copy-start.4
  1177.7 9.7 copy-start.13
  1177.7 9.7 copy-start.16
  1180.4 8.5 copy-start.6
  1180.8 5.7 collective-permute-start.5
  1182.1 5.3 collective-permute-start.4
Sparse Core Ops, SparseCore 0:
  152.6 445.2 all-reduce.5
  732.5 444.1 all-reduce.7
where the time goes:
time: 1330 us
  waiting for transfers between devices  889 us (67%)
  blocking collectives  342 us (26%)
  between operations  25.4 us (2%)
  other arithmetic  18.7 us (1%)
  starting transfers between devices  18 us (1%)
  matrix products  17.8 us (1%)
  local copies, waits for them, and re-layouts  15 us (1%)
    unnamed x4, waiting for transfers between devices  888 us
    psum x2, blocking collectives, on_device(): totals = lax.psum(local_terms, ('sub', 'grp'))  223 us
    psum x1, blocking collectives, on_device(): beta = jnp.sqrt(lax.psum(jnp.sum(first * first), ('sub', 'grp')))  119 us
  transfers between devices with their start and end apart: 8, of which 4 were waited for; matrix products, arithmetic and copies ran while one was open for 1% of the time, Pallas kernels for 0%

commit v1 on v0

v1 whole, which is shorter than its diff:
```python
import jax
import jax.numpy as jnp
from jax import lax
from jax.experimental import pallas as pl
from jax.experimental.pallas import tpu as pltpu
from jax.sharding import PartitionSpec as P

F32 = jnp.float32
BF16 = jnp.bfloat16
I32 = jnp.int32
MESH = pl.DeviceIdType.MESH

BS, NB, CPD = 64, 128, 48
NY, NZ, NG = 8, 12, 8
NSUB = NY * NZ
PLANE = NY * NG
ROWS = 3 * NY
NC = NSUB * NG * CPD
HALOS = 6
Z_ORDER = (6, 5, 7, 4, 8, 3, 9, 2, 10, 1, 11)


def iota(shape, dim):
    return lax.broadcasted_iota(I32, shape, dim)


def total(x):
    return jnp.sum(jnp.sum(x, axis=0, keepdims=True), axis=1, keepdims=True)


def kernel(
    rhs_h, guess_h, blocks_h, valve_h, jscale_h, prolong_h, agg_h, cdiag_h, coff_h, send_h, recv_h, live_h,
    sol_ref, next_ref,
    rhs, guess, blocks, valve, jscale, prolong, agg, cdiag, coff, recv, live,
    h_guess, h_prolong, h_send, h_e1, h_e2, h_sp1, h_sp2,
    plane1, plane2, plane3, line1, line2, scal1, scal2, scal3,
    onehot, link, xr, cb1, field, out_l, f_b1, f_d1, f_im1, f_b2, f_d2, e1, e2, sp1, sp2,
    load_sem, hs_sem, hr_sem, ps_sem, pr_sem, ls_sem, lr_sem,
):
    s = lax.axis_index("sub")
    g = lax.axis_index("grp")
    y = s // NZ
    z = s % NZ
    me = g * NY + y
    up = {"sub": (s + 1) % NSUB}
    down = {"sub": (s + NSUB - 1) % NSUB}

    def plane_dev(t):
        return {"sub": (t % NY) * NZ + z, "grp": t // NY}

    def line_dev(dz):
        return {"sub": y * NZ + (z + dz) % NZ}

    barrier = pltpu.get_barrier_semaphore()
    for where in (up, down):
        pl.semaphore_signal(barrier, inc=1, device_id=where, device_id_type=MESH)
    for dz in Z_ORDER:
        pl.semaphore_signal(barrier, inc=1, device_id=line_dev(dz), device_id_type=MESH)

    def greet(i, carry):
        pl.semaphore_signal(barrier, inc=1, device_id=plane_dev((me + i) % PLANE), device_id_type=MESH)
        return carry

    lax.fori_loop(1, PLANE, greet, 0)

    loads = [
        pltpu.make_async_copy(src, dst, load_sem.at[i])
        for i, (src, dst) in enumerate(
            (
                (guess_h, guess), (blocks_h, blocks), (rhs_h, rhs), (valve_h, valve), (prolong_h, prolong),
                (agg_h, agg), (recv_h, recv), (live_h, live), (jscale_h, jscale), (cdiag_h, cdiag), (coff_h, coff),
            )
        )
    ]
    for load in loads:
        load.start()

    pl.semaphore_wait(barrier, 2 + len(Z_ORDER) + PLANE - 1)

    def halo(which, src, dst):
        return [
            pltpu.make_async_remote_copy(
                src, dst.at[side], hs_sem.at[which, side], hr_sem.at[which, side],
                device_id=where, device_id_type=MESH,
            )
            for side, where in ((0, up), (1, down))
        ]

    halo_guess = halo(0, guess_h.at[0, 0], h_guess)
    halo_send = halo(1, send_h.at[0, 0], h_send)
    halo_prolong = halo(2, prolong_h.at[0, 0], h_prolong)
    halo_e1 = halo(3, e1, h_e1)
    halo_e2 = halo(4, e2, h_e2)
    halo_sp1 = halo(5, sp1, h_sp1)
    halo_sp2 = halo(6, sp2, h_sp2)
    for copy in halo_guess + halo_send + halo_prolong:
        copy.start()

    def across_plane(buf, which):
        def one(off):
            t = (me + off) % PLANE
            return pltpu.make_async_remote_copy(
                buf.at[pl.ds(me, 1)], buf.at[pl.ds(me, 1)], ps_sem.at[which], pr_sem.at[which],
                device_id=plane_dev(t), device_id_type=MESH,
            )

        def body(i, carry):
            one(i).start()
            return carry

        lax.fori_loop(PLANE // 2 + NY // 2, PLANE, body, 0)
        lax.fori_loop(1, PLANE // 2 + NY // 2, body, 0)

    def plane_all(buf, which):
        return pltpu.make_async_remote_copy(
            buf.at[pl.ds(0, PLANE - 1)], buf.at[pl.ds(0, PLANE - 1)], ps_sem.at[which], pr_sem.at[which],
            device_id=up, device_id_type=MESH,
        )

    def across_line(buf, which):
        for dz in Z_ORDER:
            pltpu.make_async_remote_copy(
                buf.at[z], buf.at[z], ls_sem.at[which], lr_sem.at[which],
                device_id=line_dev(dz), device_id_type=MESH,
            ).start()

    def line_all(buf, which):
        return pltpu.make_async_remote_copy(
            buf.at[pl.ds(0, NZ - 1)], buf.at[pl.ds(0, NZ - 1)], ls_sem.at[which], lr_sem.at[which],
            device_id=up, device_id_type=MESH,
        )

    lane = iota((1, NB), 1)
    spare = (CPD * (g + 1)) % NB

    def apply_local(v):
        def body(t, carry):
            rows = []
            for i in range(8):
                prod = blocks[0, 0, 8 * t + i].astype(F32) * v
                acc = prod[0:8]
                for j in range(1, 8):
                    acc = acc + prod[8 * j : 8 * j + 8]
                rows.append(jnp.sum(acc, axis=0, keepdims=True))
            out_l[pl.ds(pl.multiple_of(8 * t, 8), 8), :] = jnp.concatenate(rows, axis=0)
            return carry

        lax.fori_loop(0, BS // 8, body, 0)
        return out_l[...] + (3.0 * valve[0].astype(F32)) * v

    def apply_link(below, above):
        both = jnp.concatenate([below, above], axis=1)
        hi = both.astype(BF16)
        lo = (both - hi.astype(F32)).astype(BF16)
        out = jnp.dot(jnp.concatenate([hi, lo], axis=0), link[...], preferred_element_type=F32)
        return out[:BS] + out[BS:]

    def restrict(v):
        weighted = jnp.sum(prolong[0, 0] * v, axis=0, keepdims=True)
        return jnp.sum(onehot[...] * weighted, axis=1, keepdims=True)

    def message(column, scalars):
        place = iota((CPD, NB), 1) == (iota((CPD, NB), 0) + CPD * g) % NB
        row = jnp.sum(jnp.where(place, column, 0.0), axis=0, keepdims=True)
        for i, value in enumerate(scalars):
            row = jnp.where(lane == spare + i, value, row)
        return row

    def gather(plane, line, scal, which):
        across_plane(plane, which)
        plane_all(plane, which).wait_recv()
        spot = iota((NY, NB), 1)
        parts = [None] * 3
        extra = None
        for gg in range(NG):
            v = plane[NY * gg : NY * gg + NY, :]
            for k in range(3):
                lo, hi = max(CPD * gg, NB * k), min(CPD * gg + CPD, NB * k + NB)
                if lo < hi:
                    term = jnp.where((spot >= lo - NB * k) & (spot < hi - NB * k), v, 0.0)
                    parts[k] = term if parts[k] is None else parts[k] + term
            at = (CPD * (gg + 1)) % NB
            term = jnp.where((spot == at) | (spot == at + 1), v, 0.0)
            extra = term if extra is None else extra + term
        for k in range(3):
            line[z, NY * k : NY * k + NY, :] = parts[k]
        scal[z] = jnp.sum(extra, axis=0, keepdims=True)
        across_line(scal, which)
        across_line(line, 3 + which)
        line_all(scal, which).wait_recv()
        line_all(line, 3 + which).wait_recv()
        sums = jnp.sum(scal[...], axis=0)
        return [jnp.sum(jnp.where(lane % 16 == i, sums, 0.0), axis=1, keepdims=True) for i in (0, 1)]

    def coarse_product():
        def body(zz, acc):
            for k in range(3):
                for yy in range(NY):
                    at = pl.multiple_of(((yy * NZ + zz) * 3 + k) * NB, NB)
                    r = NY * k + yy
                    acc = acc + coff[:, pl.ds(at, NB)].astype(F32) * xr[zz, r : r + 1, :]
            return acc

        acc = lax.fori_loop(0, NZ, body, jnp.zeros((CPD, NB), F32))
        return jnp.sum(acc, axis=1, keepdims=True)

    def spread_of(column):
        eye = iota((CPD, CPD), 0) == iota((CPD, CPD), 1)
        diag = jnp.sum(jnp.where(eye, cdiag[...].reshape(1, CPD), 0.0), axis=1, keepdims=True)
        sol = diag * column + coarse_product()
        return jnp.sum(onehot[...] * sol, axis=0, keepdims=True)

    loads[0].wait()
    loads[1].wait()
    loads[3].wait()
    field[...] = apply_local(guess[0, 0])
    for i in (2, 4, 5, 6, 7, 8, 9):
        loads[i].wait()
    onehot[...] = jnp.where(iota((CPD, NB), 0) == agg[0], 1.0, 0.0)
    for copy in halo_send:
        copy.wait_recv()
    for side in (0, 1):
        rows_i = iota((NB, NB), 0)
        took = jnp.where(rows_i == h_send[side][side : side + 1, :], 1.0, 0.0).astype(BF16)
        alive = iota((NB, NB), 1) < live[0][:, side : side + 1]
        puts = jnp.where((rows_i == recv[0, 0][side : side + 1, :]) & alive, 1.0, 0.0).astype(BF16)
        both = lax.dot_general(took, puts, (((1,), (1,)), ((), ())), preferred_element_type=F32)
        end = 0 if side == 0 else NSUB - 1
        both = both * jnp.where(s == end, 0.0, -0.5)
        link[NB * side : NB * side + NB, :] = both.astype(BF16)
    for copy in halo_guess:
        copy.wait_recv()
    first = rhs[0, 0] - field[...] - apply_link(h_guess[0], h_guess[1])
    own1 = restrict(first)
    plane1[pl.ds(me, 1), :] = message(own1, [total(first * first), jnp.zeros((1, 1), F32)])
    e1[...] = jscale[0, 0] * first
    for copy in halo_e1:
        copy.start()
    f_b1[...] = first

    square, _ = gather(plane1, line1, scal1, 0)
    beta = jnp.sqrt(square)
    inv1 = 1.0 / beta
    for zz in range(NZ):
        x = line1[zz] * inv1
        cb1[zz] = x
        xr[zz] = x.astype(BF16).astype(F32)
    own1 = own1 * inv1
    loads[10].wait()
    spread = spread_of(own1)
    sp1[...] = spread
    for copy in halo_sp1:
        copy.start()
    f_b1[...] = f_b1[...] * inv1
    f_d1[...] = jscale[0, 0] * f_b1[...] + prolong[0, 0] * spread
    field[...] = apply_local(f_d1[...])
    for copy in halo_prolong + halo_e1 + halo_sp1:
        copy.wait_recv()
    image = field[...] + apply_link(
        *[h_e1[side] * inv1 + h_prolong[side] * h_sp1[side] for side in (0, 1)]
    )
    own2 = restrict(image)
    plane2[pl.ds(me, 1), :] = message(own2, [total(f_b1[...] * image), total(image * image)])
    e2[...] = jscale[0, 0] * image
    for copy in halo_e2:
        copy.start()
    f_im1[...] = image

    h11, energy = gather(plane2, line2, scal2, 1)
    h21 = jnp.sqrt(jnp.maximum(energy - h11 * h11, 0.01 * energy))
    inv2 = 1.0 / h21
    for zz in range(NZ):
        x = (line2[zz] - h11 * cb1[zz]) * inv2
        xr[zz] = x.astype(BF16).astype(F32)
    own2 = (own2 - h11 * own1) * inv2
    spread = spread_of(own2)
    sp2[...] = spread
    for copy in halo_sp2:
        copy.start()
    f_b2[...] = (f_im1[...] - h11 * f_b1[...]) * inv2
    f_d2[...] = jscale[0, 0] * f_b2[...] + prolong[0, 0] * spread
    field[...] = apply_local(f_d2[...])
    for copy in halo_e2 + halo_sp2:
        copy.wait_recv()
    back = h11 * inv1
    image = field[...] + apply_link(
        *[(h_e2[side] - back * h_e1[side]) * inv2 + h_prolong[side] * h_sp2[side] for side in (0, 1)]
    )

    row = jnp.zeros((1, NB), F32)
    for i, value in enumerate((total(f_b1[...] * image), total(f_b2[...] * image), total(image * image))):
        row = jnp.where(lane == i, value, row)
    plane3[pl.ds(me, 1), :] = row
    across_plane(plane3, 2)
    plane_all(plane3, 2).wait_recv()
    scal3[z] = jnp.sum(plane3[...], axis=0, keepdims=True)
    across_line(scal3, 2)
    line_all(scal3, 2).wait_recv()
    sums = jnp.sum(scal3[...], axis=0)
    h12, h22, energy = [jnp.sum(jnp.where(lane == i, sums, 0.0), axis=1, keepdims=True) for i in range(3)]
    h32 = jnp.sqrt(jnp.maximum(energy - (h12 * h12 + h22 * h22), 0.01 * energy))
    g00 = h11 * h11 + h21 * h21
    g01 = h11 * h12 + h21 * h22
    g11 = h12 * h12 + h22 * h22 + h32 * h32
    factor = g01 / g00
    t0 = beta * h11
    t1 = beta * h12 - factor * t0
    c1 = t1 / (g11 - factor * g01)
    c0 = (t0 - g01 * c1) / g00
    next_ref[0, 0] = (image - h12 * f_b1[...] - h22 * f_b2[...]) * (1.0 / h32)
    sol_ref[0, 0] = guess[0, 0] + c0 * f_d1[...] + c1 * f_d2[...]

    for copy in halo_guess + halo_send + halo_prolong + halo_e1 + halo_e2 + halo_sp1 + halo_sp2:
        copy.wait_send()
    for which, buf in enumerate((plane1, plane2, plane3)):
        plane_all(buf, which).wait_send()
    for which, buf in enumerate((scal1, scal2, scal3, line1, line2)):
        line_all(buf, which).wait_send()


def on_device(*args):
    field = (BS, NB)
    hbm_spec = pl.BlockSpec(memory_space=pltpu.HBM)
    vmem_spec = pl.BlockSpec(memory_space=pltpu.VMEM)
    sides = (2, BS, NB)
    shape = jax.ShapeDtypeStruct((1, 1, BS, NB), F32)
    return pl.pallas_call(
        kernel,
        out_shape=(shape, shape),
        in_specs=[hbm_spec] * 12,
        out_specs=(vmem_spec, vmem_spec),
        scratch_shapes=[
            *[pltpu.VMEM(args[i].shape, args[i].dtype) for i in (0, 1, 2, 3, 4, 5, 6, 7, 8, 10, 11)],
            pltpu.VMEM(sides, F32),
            pltpu.VMEM(sides, F32),
            pltpu.VMEM((2, 2, NB), I32),
            pltpu.VMEM(sides, F32),
            pltpu.VMEM(sides, F32),
            pltpu.VMEM((2, 1, NB), F32),
            pltpu.VMEM((2, 1, NB), F32),
            *[pltpu.VMEM((PLANE, NB), F32)] * 3,
            *[pltpu.VMEM((NZ, ROWS, NB), F32)] * 2,
            *[pltpu.VMEM((NZ, 1, NB), F32)] * 3,
            pltpu.VMEM((CPD, NB), F32),
            pltpu.VMEM((2 * NB, NB), BF16),
            pltpu.VMEM((NZ, ROWS, NB), F32),
            pltpu.VMEM((NZ, ROWS, NB), F32),
            *[pltpu.VMEM(field, F32)] * 9,
            pltpu.VMEM((1, NB), F32),
            pltpu.VMEM((1, NB), F32),
            pltpu.SemaphoreType.DMA((11,)),
            pltpu.SemaphoreType.DMA((7, 2)),
            pltpu.SemaphoreType.DMA((7, 2)),
            pltpu.SemaphoreType.DMA((3,)),
            pltpu.SemaphoreType.DMA((3,)),
            pltpu.SemaphoreType.DMA((5,)),
            pltpu.SemaphoreType.DMA((5,)),
        ],
        compiler_params=pltpu.CompilerParams(
            collective_id=0, has_side_effects=True, vmem_limit_bytes=61900 * 1024
        ),
    )(*args)


def solution(mesh):
    return jax.shard_map(
        on_device,
        mesh=mesh,
        in_specs=(
            P("sub", "grp", None, None),
            P("sub", "grp", None, None),
            P("sub", "grp", None, None, None),
            P("sub", "grp", None),
            P("sub", "grp", None, None),
            P("sub", "grp", None, None),
            P("sub", "grp", None),
            P(("sub", "grp")),
            P(("sub", "grp"), None),
            P("sub", "grp", None, None),
            P("sub", "grp", None, None),
            P("sub", "grp", None),
        ),
        out_specs=(P("sub", "grp", None, None), P("sub", "grp", None, None)),
        check_vma=False,
    )
```

time: 1330 us -> 79.3 us (0.06)
  waiting for transfers between devices: 889 us -> 0 us
  blocking collectives: 342 us -> 0 us
  Pallas kernels: 0 us -> 75.7 us
  between operations: 25.4 us -> 0.64 us
  other arithmetic: 18.7 us -> 0 us
  starting transfers between devices: 18 us -> 0 us
  matrix products: 17.8 us -> 0 us
    unnamed x4 -> x0, waiting for transfers between devices: 888 us -> none
    psum x3 -> x0, blocking collectives: 342 us -> none  [the longest x2 223 us: on_device(): totals = lax.psum(local_terms, ('sub', 'grp'))]
    pallas_call x0 -> x1, Pallas kernels: none -> 75.7 us  [on_device(): pl.pallas_call(kernel, out_shape=(shape, shape), in_specs=[hbm_spec] * 12...]
    ppermute x6 -> x0, starting transfers between devices: 17.9 us -> none  [the longest x3 14.1 us: extended(): lax.ppermute(tail, axis, [(i, (i + 1) % count) for i in range(ends)])]
    dot_general x19 -> x0, matrix products: 17.8 us -> none  [the longest x3 5.36 us: operate(): jnp.dot(below, recv_sel[0], precision=highest)]
  transfers between devices with their start and end apart: 8 -> 0, of which waited for: 4 -> 0; matrix products, arithmetic and copies ran while one was open for 1% -> 0% of each run, Pallas kernels for 0% -> 0%
where the time goes in v1:
time: 79.3 us; the launch traced here: 79 us
  Pallas kernels  75.7 us (95%)
  local copies, waits for them, and re-layouts  2.75 us (3%)
    pallas_call x1, Pallas kernels, on_device(): pl.pallas_call(kernel, out_shape=(shape, shape), in_specs=[hbm_spec] * 12...  75.7 us
    unnamed x2, local copies, waits for them, and re-layouts  2.75 us

profile of v1, /device:TPU:1, one launch (start us, length us, event | category | flops | bytes accessed | tf_op | source)
XLA Modules:
  0.0 79.0 jit_solution(15346604516960880005)
XLA Ops:
  0.6 75.7 %shard_map.131 = (f32[1,1,64,128]{3,2,1,0:T(8,128)}, f32[1,1,64,128]{3,2,1,0:T(8,128)}) custom-call(f32[1,1,64,128]{3,2,1,0:T(8,128)} %rhs_h.1, f32[1,1,64,128]{3,2,1,0:T(8,128)} %guess_h.1, bf16[1,1,64,64,128]{4,3,2,1,0:T(8,128)(2,1)} %blocks_h.1, s32[1,1,128]{2,1,0:T(1,128)} %valve_h.1, f32[1,1,64,128]{3,2,1,0:T(8,128)} %jscale_h.1, ...), custom_call_target="tpu_custom_call" | custom-call | tf_op jit(solution)/shard_map/pallas_call | solution.py:327
  76.3 1.4 %copy.16 = f32[1,1,64,128]{3,2,1,0:T(8,128)} copy(f32[1,1,64,128]{3,2,1,0:T(8,128)} %get-tuple-element.4) | data formatting | bytes 65536
  77.7 1.4 %copy.17 = f32[1,1,64,128]{3,2,1,0:T(8,128)} copy(f32[1,1,64,128]{3,2,1,0:T(8,128)} %get-tuple-element.5) | data formatting | bytes 65536

commit v2 on v1

v2 whole, which is shorter than its diff:
```python
import jax
import jax.numpy as jnp
from jax import lax
from jax.experimental import pallas as pl
from jax.experimental.pallas import tpu as pltpu
from jax.sharding import PartitionSpec as P

F32 = jnp.float32
BF16 = jnp.bfloat16
I32 = jnp.int32
MESH = pl.DeviceIdType.MESH

BS, NB, CPD = 64, 128, 48
NY, NZ, NG = 8, 12, 8
NSUB = NY * NZ
PLANE = NY * NG
NC = NSUB * NG * CPD
NEAR = (0, 1, 2, 7)
HALF = 12
Z_ORDER = (6, 5, 7, 4, 8, 3, 9, 2, 10, 1, 11)


def iota(shape, dim):
    return lax.broadcasted_iota(I32, shape, dim)


def total(x):
    return jnp.sum(jnp.sum(x, axis=0, keepdims=True), axis=1, keepdims=True)


def kernel(
    rhs_h, guess_h, blocks_h, valve_h, jscale_h, prolong_h, agg_h, cdiag_h, coff_h, send_h, recv_h, live_h,
    sol_ref, next_ref,
    rhs, guess, blocks, valve, jscale, prolong, agg, cdiag, coff, recv, live,
    h_guess, h_prolong, h_send, h_e1, h_e2, h_sp1, h_sp2,
    plane1, plane2, plane3, line1, line2, scal3,
    onehot, place, diag, link, wide, xs, cs, field, out_l, f_b1, f_d1, f_im1, f_b2, f_d2, e1, e2, sp1, sp2,
    load_sem, hs_sem, hr_sem, ps_sem, pr_sem, ls_sem, lr_sem, fs_sem, fr_sem, cs_sem, cr_sem, sync,
):
    s = lax.axis_index("sub")
    g = lax.axis_index("grp")
    y = s // NZ
    z = s % NZ
    me = g * NY + y
    mine = NY * g + 2
    core = g % 2
    sibling = {"grp": g + 1 - 2 * core}
    up = {"sub": (s + 1) % NSUB}
    down = {"sub": (s + NSUB - 1) % NSUB}

    def plane_dev(t):
        return {"sub": (t % NY) * NZ + z, "grp": t // NY}

    def line_dev(dz):
        return {"sub": y * NZ + (z + dz) % NZ}

    barrier = pltpu.get_barrier_semaphore()

    def greet(where):
        pl.semaphore_signal(barrier, inc=1, device_id=where, device_id_type=MESH)

    for where in (up, down):
        greet({**where, "grp": g + 1 - core})

    @pl.when(core == 0)
    def _():
        greet(sibling)

    def greet_plane(t, carry):
        greet({"sub": ((y + t // 4) % NY) * NZ + z, "grp": ((g // 2 + t) % 4) * 2})
        return carry

    def greet_line(i, carry):
        greet({"sub": y * NZ + (z + i) % NZ, "grp": g - core})
        return carry

    lax.fori_loop(16, 32, greet_plane, 0)
    lax.fori_loop(1, NZ, greet_line, 0)
    lax.fori_loop(1, 16, greet_plane, 0)

    @pl.when(core == 1)
    def _():
        greet(sibling)

    loads = [
        pltpu.make_async_copy(src, dst, load_sem.at[i])
        for i, (src, dst) in enumerate(
            (
                (guess_h, guess), (blocks_h, blocks), (rhs_h, rhs), (valve_h, valve), (prolong_h, prolong),
                (agg_h, agg), (recv_h, recv), (live_h, live), (jscale_h, jscale), (cdiag_h, cdiag), (coff_h, coff),
            )
        )
    ]
    for load in loads:
        load.start()

    loads[0].wait()
    loads[4].wait()

    @pl.when(core == 1)
    def _():
        pl.semaphore_wait(barrier, 5)
        pl.semaphore_signal(sync, inc=1, device_id=sibling, device_id_type=MESH)

    @pl.when(core == 0)
    def _():
        pl.semaphore_wait(sync, 1)

    def halo(which, src, dst):
        return [
            pltpu.make_async_remote_copy(
                src, dst.at[side], hs_sem.at[which, side], hr_sem.at[which, side],
                device_id=where, device_id_type=MESH,
            )
            for side, where in ((0, up), (1, down))
        ]

    halo_guess = halo(0, guess.at[0, 0], h_guess)
    halo_send = halo(1, send_h.at[0, 0], h_send)
    halo_prolong = halo(2, prolong.at[0, 0], h_prolong)
    halo_e1 = halo(3, e1, h_e1)
    halo_e2 = halo(4, e2, h_e2)
    halo_sp1 = halo(5, sp1, h_sp1)
    halo_sp2 = halo(6, sp2, h_sp2)
    for copy in halo_guess + halo_send + halo_prolong:
        copy.start()

    def across_plane(buf, which):
        for oy in (4, 3, 5, 2, 6, 1, 7, 0):
            cls = 0 if oy in NEAR else 1

            def one(i, carry):
                pltpu.make_async_remote_copy(
                    buf.at[pl.ds(mine, 1)], buf.at[pl.ds(NY * g + (2 - oy) % NY, 1)],
                    ps_sem.at[which, cls], pr_sem.at[which, cls],
                    device_id={"sub": ((y + oy) % NY) * NZ + z, "grp": (g + i) % NG}, device_id_type=MESH,
                ).start()
                return carry

            lax.fori_loop(4, NG, one, 0)
            lax.fori_loop(0 if oy else 1, 4, one, 0)

    def plane_all(buf, which, cls):
        count = NG * 4 - 1 if cls == 0 else NG * 4
        return pltpu.make_async_remote_copy(
            buf.at[pl.ds(0, count)], buf.at[pl.ds(0, count)], ps_sem.at[which, cls], pr_sem.at[which, cls],
            device_id=up, device_id_type=MESH,
        )

    def line_copy(buf, dz, which):
        return pltpu.make_async_remote_copy(
            buf.at[core, z], buf.at[core, z], ls_sem.at[which, dz], lr_sem.at[which, dz],
            device_id=line_dev(dz), device_id_type=MESH,
        )

    def hand_over(buf, dz, which):
        at = (z + NZ - dz) % NZ
        return pltpu.make_async_remote_copy(
            buf.at[core, at], buf.at[core, at], fs_sem.at[which], fr_sem.at[which],
            device_id=sibling, device_id_type=MESH,
        )

    def handed_over(buf, which):
        return pltpu.make_async_remote_copy(
            buf.at[0, pl.ds(0, NZ - 1)], buf.at[0, pl.ds(0, NZ - 1)], fs_sem.at[which], fr_sem.at[which],
            device_id=sibling, device_id_type=MESH,
        )

    def scal_copy(dz):
        return pltpu.make_async_remote_copy(
            scal3.at[z], scal3.at[z], cs_sem, cr_sem, device_id=line_dev(dz), device_id_type=MESH,
        )

    scal_all = pltpu.make_async_remote_copy(
        scal3.at[pl.ds(0, NZ - 1)], scal3.at[pl.ds(0, NZ - 1)], cs_sem, cr_sem, device_id=up, device_id_type=MESH,
    )

    lane = iota((1, NB), 1)
    spare = (CPD * (g + 1)) & (NB - 1)

    def apply_local(v):
        def body(t, carry):
            rows = []
            for i in range(8):
                prod = blocks[0, 0, 8 * t + i].astype(F32) * v
                acc = prod[0:8]
                for j in range(1, 8):
                    acc = acc + prod[8 * j : 8 * j + 8]
                rows.append(jnp.sum(acc, axis=0, keepdims=True))
            out_l[pl.ds(pl.multiple_of(8 * t, 8), 8), :] = jnp.concatenate(rows, axis=0)
            return carry

        lax.fori_loop(0, BS // 8, body, 0)
        return out_l[...] + (3.0 * valve[0].astype(F32)) * v

    def apply_link(below, above):
        both = jnp.concatenate([below, above], axis=1)
        hi = both.astype(BF16)
        lo = (both - hi.astype(F32)).astype(BF16)
        out = jnp.dot(jnp.concatenate([hi, lo], axis=0), link[...], preferred_element_type=F32)
        return out[:BS] + out[BS:]

    def restrict(v):
        weighted = jnp.sum(prolong[0, 0] * v, axis=0, keepdims=True)
        return jnp.sum(onehot[...] * weighted, axis=1, keepdims=True)

    def message(column, scalars):
        row = jnp.sum(place[...] * column, axis=0, keepdims=True)
        for i, value in enumerate(scalars):
            row = jnp.where(lane == spare + i, value, row)
        return row

    def pick(plane, first_row, count):
        spot = iota((count, NB), 1)
        parts = [None] * 3
        extra = None
        for gg in range(NG):
            v = plane[NY * gg + first_row : NY * gg + first_row + count, :]
            for k in range(3):
                lo, hi = max(CPD * gg, NB * k), min(CPD * gg + CPD, NB * k + NB)
                if lo < hi:
                    term = jnp.where((spot >= lo - NB * k) & (spot < hi - NB * k), v, 0.0)
                    parts[k] = term if parts[k] is None else parts[k] + term
            at = (CPD * (gg + 1)) % NB
            term = jnp.where((spot == at) | (spot == at + 1), v, 0.0)
            extra = term if extra is None else extra + term
        return parts, jnp.sum(extra, axis=0, keepdims=True)

    def gather(plane, line, which):
        def send_own():
            for dz in Z_ORDER:
                line_copy(line, dz, which).start()

        plane_all(plane, which, 0).wait_recv()
        parts, some = pick(plane, 0, 4)
        for k in range(3):
            line[0, z, 4 * k : 4 * k + 4, :] = parts[k]
        line[0, z, HALF : HALF + 1, :] = jnp.zeros((1, NB), F32)
        pl.when(core == 0)(send_own)
        plane_all(plane, which, 1).wait_recv()
        parts, rest = pick(plane, 4, 4)
        for k in range(3):
            line[1, z, 4 * k : 4 * k + 4, :] = parts[k]
        line[1, z, HALF : HALF + 1, :] = some + rest
        pl.when(core == 1)(send_own)
        for dz in reversed(Z_ORDER):
            line_copy(line, dz, which).wait_recv()
            hand_over(line, dz, which).start()
        handed_over(line, which).wait_recv()
        sums = jnp.sum(line[1, :, HALF, :], axis=0, keepdims=True)
        return [jnp.sum(jnp.where(lane & 15 == i, sums, 0.0), axis=1, keepdims=True) for i in (0, 1)]

    def coarse_product():
        def body(zz, acc):
            for r in range(NY):
                base = (((y + r + NY - 2) % NY) * NZ + zz) * 3
                for k in range(3):
                    at = pl.multiple_of((base + k) * NB, NB)
                    row = 4 * k + r % 4
                    acc = acc + wide[:, pl.ds(at, NB)] * xs[r // 4, zz, row : row + 1, :]
            return acc

        acc = lax.fori_loop(0, NZ, body, jnp.zeros((CPD, NB), F32))
        return jnp.sum(acc, axis=1, keepdims=True)

    def spread_of(column):
        sol = diag[:, 0:1] * column + coarse_product()
        return jnp.sum(onehot[...] * sol, axis=0, keepdims=True)

    loads[1].wait()
    loads[3].wait()
    field[...] = apply_local(guess[0, 0])
    for i in (2, 5, 6, 7, 8, 9):
        loads[i].wait()
    onehot[...] = jnp.where(iota((CPD, NB), 0) == agg[0], 1.0, 0.0)
    place[...] = jnp.where(iota((CPD, NB), 1) == (iota((CPD, NB), 0) + CPD * g) & (NB - 1), 1.0, 0.0)
    eye = iota((CPD, CPD), 0) == iota((CPD, CPD), 1)
    diag[...] = jnp.zeros((CPD, NB), F32) + jnp.sum(
        jnp.where(eye, cdiag[...].reshape(1, CPD), 0.0), axis=1, keepdims=True
    )
    for copy in halo_send:
        copy.wait_recv()
    for side in (0, 1):
        rows_i = iota((NB, NB), 0)
        took = jnp.where(rows_i == h_send[side][side : side + 1, :], 1.0, 0.0).astype(BF16)
        alive = iota((NB, NB), 1) < live[0][:, side : side + 1]
        puts = jnp.where((rows_i == recv[0, 0][side : side + 1, :]) & alive, 1.0, 0.0).astype(BF16)
        both = lax.dot_general(took, puts, (((1,), (1,)), ((), ())), preferred_element_type=F32)
        end = 0 if side == 0 else NSUB - 1
        both = both * jnp.where(s == end, 0.0, -0.5)
        link[NB * side : NB * side + NB, :] = both.astype(BF16)

    @pl.when(core == 0)
    def _():
        pl.semaphore_wait(barrier, PLANE - 1 + 2 * (NZ - 1))
        pl.semaphore_signal(sync, inc=1, device_id=sibling, device_id_type=MESH)

    for copy in halo_guess:
        copy.wait_recv()
    first = rhs[0, 0] - field[...] - apply_link(h_guess[0], h_guess[1])
    own1 = restrict(first)
    plane1[pl.ds(mine, 1), :] = message(own1, [total(first * first), jnp.zeros((1, 1), F32)])

    @pl.when(core == 1)
    def _():
        pl.semaphore_wait(sync, 1)

    across_plane(plane1, 0)
    e1[...] = jscale[0, 0] * first
    for copy in halo_e1:
        copy.start()
    f_b1[...] = first
    loads[10].wait()

    def widen(i, carry):
        at = pl.multiple_of(i * 8 * NB, NB)
        wide[:, pl.ds(at, 8 * NB)] = coff[:, pl.ds(at, 8 * NB)].astype(F32)
        return carry

    lax.fori_loop(0, NC // (8 * NB), widen, 0)

    square, _ = gather(plane1, line1, 0)
    beta = jnp.sqrt(square)
    inv1 = 1.0 / beta
    for zz in range(NZ):
        for half in (0, 1):
            x = line1[half, zz, 0:HALF, :] * inv1
            cs[half, zz] = x
            xs[half, zz] = x.astype(BF16).astype(F32)
    own1 = own1 * inv1
    spread = spread_of(own1)
    sp1[...] = spread
    for copy in halo_sp1:
        copy.start()
    f_b1[...] = f_b1[...] * inv1
    f_d1[...] = jscale[0, 0] * f_b1[...] + prolong[0, 0] * spread
    field[...] = apply_local(f_d1[...])
    for copy in halo_prolong + halo_e1 + halo_sp1:
        copy.wait_recv()
    image = field[...] + apply_link(
        *[h_e1[side] * inv1 + h_prolong[side] * h_sp1[side] for side in (0, 1)]
    )
    own2 = restrict(image)
    plane2[pl.ds(mine, 1), :] = message(own2, [total(f_b1[...] * image), total(image * image)])
    across_plane(plane2, 1)
    e2[...] = jscale[0, 0] * image
    for copy in halo_e2:
        copy.start()
    f_im1[...] = image

    h11, energy = gather(plane2, line2, 1)
    h21 = jnp.sqrt(jnp.maximum(energy - h11 * h11, 0.01 * energy))
    inv2 = 1.0 / h21
    for zz in range(NZ):
        for half in (0, 1):
            x = (line2[half, zz, 0:HALF, :] - h11 * cs[half, zz]) * inv2
            xs[half, zz] = x.astype(BF16).astype(F32)
    own2 = (own2 - h11 * own1) * inv2
    spread = spread_of(own2)
    sp2[...] = spread
    for copy in halo_sp2:
        copy.start()
    f_b2[...] = (f_im1[...] - h11 * f_b1[...]) * inv2
    f_d2[...] = jscale[0, 0] * f_b2[...] + prolong[0, 0] * spread
    field[...] = apply_local(f_d2[...])
    for copy in halo_e2 + halo_sp2:
        copy.wait_recv()
    back = h11 * inv1
    image = field[...] + apply_link(
        *[(h_e2[side] - back * h_e1[side]) * inv2 + h_prolong[side] * h_sp2[side] for side in (0, 1)]
    )

    row = jnp.zeros((1, NB), F32)
    for i, value in enumerate((total(f_b1[...] * image), total(f_b2[...] * image), total(image * image))):
        row = jnp.where(lane == i, value, row)
    plane3[pl.ds(mine, 1), :] = row
    across_plane(plane3, 2)
    g00 = h11 * h11 + h21 * h21
    inv00 = 1.0 / g00
    t0 = beta * h11
    plane_all(plane3, 2, 0).wait_recv()
    plane_all(plane3, 2, 1).wait_recv()
    scal3[z] = jnp.sum(plane3[...], axis=0, keepdims=True)
    for dz in Z_ORDER:
        scal_copy(dz).start()
    scal_all.wait_recv()
    sums = jnp.sum(scal3[...], axis=0)
    h12, h22, energy = [jnp.sum(jnp.where(lane == i, sums, 0.0), axis=1, keepdims=True) for i in range(3)]
    h32 = jnp.sqrt(jnp.maximum(energy - (h12 * h12 + h22 * h22), 0.01 * energy))
    g01 = h11 * h12 + h21 * h22
    g11 = h12 * h12 + h22 * h22 + h32 * h32
    factor = g01 * inv00
    t1 = beta * h12 - factor * t0
    c1 = t1 / (g11 - factor * g01)
    c0 = (t0 - g01 * c1) * inv00
    next_ref[0, 0] = (image - h12 * f_b1[...] - h22 * f_b2[...]) * (1.0 / h32)
    sol_ref[0, 0] = guess[0, 0] + c0 * f_d1[...] + c1 * f_d2[...]

    for copy in halo_guess + halo_send + halo_prolong + halo_e1 + halo_e2 + halo_sp1 + halo_sp2:
        copy.wait_send()
    for which, buf in enumerate((plane1, plane2, plane3)):
        for cls in (0, 1):
            plane_all(buf, which, cls).wait_send()
    for which, buf in enumerate((line1, line2)):
        for dz in Z_ORDER:
            line_copy(buf, dz, which).wait_send()
        handed_over(buf, which).wait_send()
    scal_all.wait_send()


def on_device(*args):
    field = (BS, NB)
    hbm_spec = pl.BlockSpec(memory_space=pltpu.HBM)
    vmem_spec = pl.BlockSpec(memory_space=pltpu.VMEM)
    sides = (2, BS, NB)
    shape = jax.ShapeDtypeStruct((1, 1, BS, NB), F32)
    return pl.pallas_call(
        kernel,
        out_shape=(shape, shape),
        in_specs=[hbm_spec] * 12,
        out_specs=(vmem_spec, vmem_spec),
        scratch_shapes=[
            *[pltpu.VMEM(args[i].shape, args[i].dtype) for i in (0, 1, 2, 3, 4, 5, 6, 7, 8, 10, 11)],
            pltpu.VMEM(sides, F32),
            pltpu.VMEM(sides, F32),
            pltpu.VMEM((2, 2, NB), I32),
            pltpu.VMEM(sides, F32),
            pltpu.VMEM(sides, F32),
            pltpu.VMEM((2, 1, NB), F32),
            pltpu.VMEM((2, 1, NB), F32),
            *[pltpu.VMEM((PLANE, NB), F32)] * 3,
            *[pltpu.VMEM((2, NZ, HALF + 1, NB), F32)] * 2,
            pltpu.VMEM((NZ, 1, NB), F32),
            *[pltpu.VMEM((CPD, NB), F32)] * 3,
            pltpu.VMEM((2 * NB, NB), BF16),
            pltpu.VMEM((CPD, NC), F32),
            *[pltpu.VMEM((2, NZ, HALF, NB), F32)] * 2,
            *[pltpu.VMEM(field, F32)] * 9,
            pltpu.VMEM((1, NB), F32),
            pltpu.VMEM((1, NB), F32),
            pltpu.SemaphoreType.DMA((11,)),
            pltpu.SemaphoreType.DMA((7, 2)),
            pltpu.SemaphoreType.DMA((7, 2)),
            pltpu.SemaphoreType.DMA((3, 2)),
            pltpu.SemaphoreType.DMA((3, 2)),
            pltpu.SemaphoreType.DMA((2, NZ)),
            pltpu.SemaphoreType.DMA((2, NZ)),
            pltpu.SemaphoreType.DMA((2,)),
            pltpu.SemaphoreType.DMA((2,)),
            pltpu.SemaphoreType.DMA,
            pltpu.SemaphoreType.DMA,
            pltpu.SemaphoreType.REGULAR,
        ],
        compiler_params=pltpu.CompilerParams(
            collective_id=0, has_side_effects=True, vmem_limit_bytes=40 * 1024 * 1024
        ),
    )(*[pltpu.with_memory_space_constraint(a, pltpu.HBM) for a in args])


def solution(mesh):
    return jax.shard_map(
        on_device,
        mesh=mesh,
        in_specs=(
            P("sub", "grp", None, None),
            P("sub", "grp", None, None),
            P("sub", "grp", None, None, None),
            P("sub", "grp", None),
            P("sub", "grp", None, None),
            P("sub", "grp", None, None),
            P("sub", "grp", None),
            P(("sub", "grp")),
            P(("sub", "grp"), None),
            P("sub", "grp", None, None),
            P("sub", "grp", None, None),
            P("sub", "grp", None),
        ),
        out_specs=(P("sub", "grp", None, None), P("sub", "grp", None, None)),
        check_vma=False,
    )
```

time: 79.3 us -> 69.8 us (0.88)
  Pallas kernels: 75.7 us -> 67.8 us
  local copies, waits for them, and re-layouts: 2.75 us -> 1.23 us
    pallas_call x1, Pallas kernels: 75.7 us -> 67.8 us  [on_device(): pl.pallas_call(kernel, out_shape=(shape, shape), in_specs=[hbm_spec] * 12...]
    unnamed x2, local copies, waits for them, and re-layouts: 2.75 us -> 1.23 us
where the time goes in v2:
time: 69.8 us; the launch traced here: 69.7 us
  Pallas kernels  67.8 us (97%)
  local copies, waits for them, and re-layouts  1.23 us (2%)
    pallas_call x1, Pallas kernels, on_device(): pl.pallas_call(kernel, out_shape=(shape, shape), in_specs=[hbm_spec] * 12...  67.8 us

profile of v2, /device:TPU:1, one launch (start us, length us, event | category | flops | bytes accessed | tf_op | source)
XLA Modules:
  0.0 69.7 jit_solution(13386548370059770338)
XLA Ops:
  0.6 67.8 %shard_map.131 = (f32[1,1,64,128]{3,2,1,0:T(8,128)S(1)}, f32[1,1,64,128]{3,2,1,0:T(8,128)S(1)}) custom-call(f32[1,1,64,128]{3,2,1,0:T(8,128)} %rhs_h.1, f32[1,1,64,128]{3,2,1,0:T(8,128)} %guess_h.1, bf16[1,1,64,64,128]{4,3,2,1,0:T(8,128)(2,1)} %blocks_h.1, s32[1,1,128]{2,1,0:T(1,128)} %valve_h.1, f32[1,1,64,128]{3,2,1,0:T(8,128)} %jscale_h.1, ...), custom_call_target="tpu_custom_call" | custom-call | tf_op jit(solution)/shard_map/pallas_call | solution.py:417
  68.4 0.6 copy.16
  69.0 0.6 copy.17

commit v3 on v2

--- a/solution.py
+++ b/solution.py
@@ -17,6 +17,25 @@
 NC = NSUB * NG * CPD
 NEAR = (0, 1, 2, 7)
 HALF = 12
+REACH = {6: 3, 5: 4, 4: 5}
+
+
+def hops(n, size):
+    n %= size
+    return min(n, size - n)
+
+
+CHIPS = sorted(((ox, oy) for ox in range(4) for oy in range(NY)), key=lambda o: hops(o[0], 4) + hops(o[1], NY))
+COUNTS = [20, 7, 4, 1]
+DIRECT = sorted(
+    (
+        (hops(ox, 4) + hops(oy, NY) + hops(oz, NZ), ox, oy, oz)
+        for ox, oy in CHIPS
+        for oz in range(NZ)
+        if hops(ox, 4) + hops(oy, NY) > REACH.get(hops(oz, NZ), 6)
+    ),
+    reverse=True,
+)
 Z_ORDER = (6, 5, 7, 4, 8, 3, 9, 2, 10, 1, 11)
 
 
@@ -33,9 +52,9 @@
     sol_ref, next_ref,
     rhs, guess, blocks, valve, jscale, prolong, agg, cdiag, coff, recv, live,
     h_guess, h_prolong, h_send, h_e1, h_e2, h_sp1, h_sp2,
-    plane1, plane2, plane3, line1, line2, scal3,
+    plane1, plane2, plane3, direct, part3, line1, line2, scal3,
     onehot, place, diag, link, wide, xs, cs, field, out_l, f_b1, f_d1, f_im1, f_b2, f_d2, e1, e2, sp1, sp2,
-    load_sem, hs_sem, hr_sem, ps_sem, pr_sem, ls_sem, lr_sem, fs_sem, fr_sem, cs_sem, cr_sem, sync,
+    load_sem, hs_sem, hr_sem, ps_sem, pr_sem, ls_sem, lr_sem, fs_sem, fr_sem, cs_sem, cr_sem, ds_sem, dr_sem, sync,
 ):
     s = lax.axis_index("sub")
     g = lax.axis_index("grp")
@@ -167,9 +186,49 @@
         )
 
     def scal_copy(dz):
+        cls = max(6 - hops(dz, NZ), 0)
         return pltpu.make_async_remote_copy(
-            scal3.at[z], scal3.at[z], cs_sem, cr_sem, device_id=line_dev(dz), device_id_type=MESH,
-        )
+            part3.at[min(cls, 3)], scal3.at[z], cs_sem, cr_sem, device_id=line_dev(dz), device_id_type=MESH,
+        )
+
+    def send_direct(first, last):
+        for at in range(first, last):
+            _, ox, oy, oz = DIRECT[at]
+            for flip in (0, 1):
+                pltpu.make_async_remote_copy(
+                    part3.at[4], direct.at[2 * at + core], ds_sem, dr_sem,
+                    device_id={
+                        "sub": ((y + oy) % NY) * NZ + (z + oz) % NZ,
+                        "grp": ((g // 2 + ox) % 4) * 2 + (core + flip) % 2,
+                    },
+                    device_id_type=MESH,
+                ).start()
+
+    def send_plane3():
+        for at in reversed(range(PLANE // 2)):
+            ox, oy = CHIPS[at]
+            cls = sum(at >= sum(COUNTS[: i + 1]) for i in range(3))
+            for flip in (0, 1):
+                if at or flip:
+                    pltpu.make_async_remote_copy(
+                        part3.at[4], plane3.at[2 * at + core], ps_sem.at[2, cls], pr_sem.at[2, cls],
+                        device_id={
+                            "sub": ((y + oy) % NY) * NZ + z,
+                            "grp": ((g // 2 + ox) % 4) * 2 + (core + flip) % 2,
+                        },
+                        device_id_type=MESH,
+                    ).start()
+
+    def plane3_all(cls):
+        count = 2 * COUNTS[cls] - (cls == 0)
+        return pltpu.make_async_remote_copy(
+            plane3.at[pl.ds(0, count)], plane3.at[pl.ds(0, count)], ps_sem.at[2, cls], pr_sem.at[2, cls],
+            device_id=up, device_id_type=MESH,
+        )
+
+    direct_all = pltpu.make_async_remote_copy(
+        direct, direct, ds_sem, dr_sem, device_id=up, device_id_type=MESH,
+    )
 
     scal_all = pltpu.make_async_remote_copy(
         scal3.at[pl.ds(0, NZ - 1)], scal3.at[pl.ds(0, NZ - 1)], cs_sem, cr_sem, device_id=up, device_id_type=MESH,
@@ -255,9 +314,8 @@
             for r in range(NY):
                 base = (((y + r + NY - 2) % NY) * NZ + zz) * 3
                 for k in range(3):
-                    at = pl.multiple_of((base + k) * NB, NB)
                     row = 4 * k + r % 4
-                    acc = acc + wide[:, pl.ds(at, NB)] * xs[r // 4, zz, row : row + 1, :]
+                    acc = acc + wide[base + k] * xs[r // 4, zz, row : row + 1, :]
             return acc
 
         acc = lax.fori_loop(0, NZ, body, jnp.zeros((CPD, NB), F32))
@@ -313,8 +371,9 @@
     loads[10].wait()
 
     def widen(i, carry):
-        at = pl.multiple_of(i * 8 * NB, NB)
-        wide[:, pl.ds(at, 8 * NB)] = coff[:, pl.ds(at, 8 * NB)].astype(F32)
+        for j in range(8):
+            at = pl.multiple_of((i * 8 + j) * NB, NB)
+            wide[i * 8 + j] = coff[:, pl.ds(at, NB)].astype(F32)
         return carry
 
     lax.fori_loop(0, NC // (8 * NB), widen, 0)
@@ -373,18 +432,29 @@
     row = jnp.zeros((1, NB), F32)
     for i, value in enumerate((total(f_b1[...] * image), total(f_b2[...] * image), total(image * image))):
         row = jnp.where(lane == i, value, row)
-    plane3[pl.ds(mine, 1), :] = row
-    across_plane(plane3, 2)
+    part3[4] = row
+    plane3[core] = row
+    send_direct(0, 7)
+    send_plane3()
+    send_direct(7, len(DIRECT))
     g00 = h11 * h11 + h21 * h21
     inv00 = 1.0 / g00
     t0 = beta * h11
-    plane_all(plane3, 2, 0).wait_recv()
-    plane_all(plane3, 2, 1).wait_recv()
-    scal3[z] = jnp.sum(plane3[...], axis=0, keepdims=True)
-    for dz in Z_ORDER:
-        scal_copy(dz).start()
+    some = None
+    for cls in range(4):
+        plane3_all(cls).wait_recv()
+        first_row = 2 * sum(COUNTS[:cls])
+        more = jnp.sum(plane3[first_row : first_row + 2 * COUNTS[cls]], axis=0)
+        some = more if some is None else some + more
+        part3[cls] = some
+        for dz in Z_ORDER:
+            if min(6 - hops(dz, NZ), 3) == cls:
+                scal_copy(dz).start()
+    scal3[z] = some
+    direct_all.wait_recv()
+    far_sum = jnp.sum(direct[...], axis=0)
     scal_all.wait_recv()
-    sums = jnp.sum(scal3[...], axis=0)
+    sums = jnp.sum(scal3[...], axis=0) + far_sum
     h12, h22, energy = [jnp.sum(jnp.where(lane == i, sums, 0.0), axis=1, keepdims=True) for i in range(3)]
     h32 = jnp.sqrt(jnp.maximum(energy - (h12 * h12 + h22 * h22), 0.01 * energy))
     g01 = h11 * h12 + h21 * h22
@@ -398,9 +468,12 @@
 
     for copy in halo_guess + halo_send + halo_prolong + halo_e1 + halo_e2 + halo_sp1 + halo_sp2:
         copy.wait_send()
-    for which, buf in enumerate((plane1, plane2, plane3)):
+    for which, buf in enumerate((plane1, plane2)):
         for cls in (0, 1):
             plane_all(buf, which, cls).wait_send()
+    for cls in range(4):
+        plane3_all(cls).wait_send()
+    direct_all.wait_send()
     for which, buf in enumerate((line1, line2)):
         for dz in Z_ORDER:
             line_copy(buf, dz, which).wait_send()
@@ -428,12 +501,15 @@
             pltpu.VMEM(sides, F32),
             pltpu.VMEM((2, 1, NB), F32),
             pltpu.VMEM((2, 1, NB), F32),
-            *[pltpu.VMEM((PLANE, NB), F32)] * 3,
+            *[pltpu.VMEM((PLANE, NB), F32)] * 2,
+            pltpu.VMEM((PLANE, 1, NB), F32),
+            pltpu.VMEM((2 * len(DIRECT), 1, NB), F32),
+            pltpu.VMEM((5, 1, NB), F32),
             *[pltpu.VMEM((2, NZ, HALF + 1, NB), F32)] * 2,
             pltpu.VMEM((NZ, 1, NB), F32),
             *[pltpu.VMEM((CPD, NB), F32)] * 3,
             pltpu.VMEM((2 * NB, NB), BF16),
-            pltpu.VMEM((CPD, NC), F32),
+            pltpu.VMEM((NC // NB, CPD, NB), F32),
             *[pltpu.VMEM((2, NZ, HALF, NB), F32)] * 2,
             *[pltpu.VMEM(field, F32)] * 9,
             pltpu.VMEM((1, NB), F32),
@@ -441,14 +517,13 @@
             pltpu.SemaphoreType.DMA((11,)),
             pltpu.SemaphoreType.DMA((7, 2)),
             pltpu.SemaphoreType.DMA((7, 2)),
-            pltpu.SemaphoreType.DMA((3, 2)),
-            pltpu.SemaphoreType.DMA((3, 2)),
+            pltpu.SemaphoreType.DMA((3, 4)),
+            pltpu.SemaphoreType.DMA((3, 4)),
             pltpu.SemaphoreType.DMA((2, NZ)),
             pltpu.SemaphoreType.DMA((2, NZ)),
             pltpu.SemaphoreType.DMA((2,)),
             pltpu.SemaphoreType.DMA((2,)),
-            pltpu.SemaphoreType.DMA,
-            pltpu.SemaphoreType.DMA,
+            *[pltpu.SemaphoreType.DMA] * 4,
             pltpu.SemaphoreType.REGULAR,
         ],
         compiler_params=pltpu.CompilerParams(

time: 69.8 us -> 68.4 us (0.980)
  Pallas kernels: 67.8 us -> 66.4 us
    pallas_call x1, Pallas kernels: 67.8 us -> 66.4 us  [on_device(): pl.pallas_call(kernel, out_shape=(shape, shape), in_specs=[hbm_spec] * 12...]
where the time goes in v3:
time: 68.4 us; the launch traced here: 68.2 us
  Pallas kernels  66.4 us (97%)
  local copies, waits for them, and re-layouts  1.23 us (2%)
    pallas_call x1, Pallas kernels, on_device(): pl.pallas_call(kernel, out_shape=(shape, shape), in_specs=[hbm_spec] * 12...  66.4 us

profile of v3, /device:TPU:1, one launch (start us, length us, event | category | flops | bytes accessed | tf_op | source)
XLA Modules:
  0.0 68.2 jit_solution(15686231973727302679)
XLA Ops:
  0.6 66.4 %shard_map.131 = (f32[1,1,64,128]{3,2,1,0:T(8,128)S(1)}, f32[1,1,64,128]{3,2,1,0:T(8,128)S(1)}) custom-call(f32[1,1,64,128]{3,2,1,0:T(8,128)} %rhs_h.1, f32[1,1,64,128]{3,2,1,0:T(8,128)} %guess_h.1, bf16[1,1,64,64,128]{4,3,2,1,0:T(8,128)(2,1)} %blocks_h.1, s32[1,1,128]{2,1,0:T(1,128)} %valve_h.1, f32[1,1,64,128]{3,2,1,0:T(8,128)} %jscale_h.1, ...), custom_call_target="tpu_custom_call" | custom-call | tf_op jit(solution)/shard_map/pallas_call | solution.py:490
  67.0 0.6 copy.16
  67.6 0.6 copy.17

commit v4 on v3

--- a/solution.py
+++ b/solution.py
@@ -49,7 +49,7 @@
 
 def kernel(
     rhs_h, guess_h, blocks_h, valve_h, jscale_h, prolong_h, agg_h, cdiag_h, coff_h, send_h, recv_h, live_h,
-    sol_ref, next_ref,
+    out_ref,
     rhs, guess, blocks, valve, jscale, prolong, agg, cdiag, coff, recv, live,
     h_guess, h_prolong, h_send, h_e1, h_e2, h_sp1, h_sp2,
     plane1, plane2, plane3, direct, part3, line1, line2, scal3,
@@ -141,7 +141,7 @@
     halo_e2 = halo(4, e2, h_e2)
     halo_sp1 = halo(5, sp1, h_sp1)
     halo_sp2 = halo(6, sp2, h_sp2)
-    for copy in halo_guess + halo_send + halo_prolong:
+    for copy in halo_send + halo_guess + halo_prolong:
         copy.start()
 
     def across_plane(buf, which):
@@ -204,8 +204,8 @@
                     device_id_type=MESH,
                 ).start()
 
-    def send_plane3():
-        for at in reversed(range(PLANE // 2)):
+    def send_plane3(chips):
+        for at in chips:
             ox, oy = CHIPS[at]
             cls = sum(at >= sum(COUNTS[: i + 1]) for i in range(3))
             for flip in (0, 1):
@@ -336,16 +336,17 @@
     diag[...] = jnp.zeros((CPD, NB), F32) + jnp.sum(
         jnp.where(eye, cdiag[...].reshape(1, CPD), 0.0), axis=1, keepdims=True
     )
+    rows_i = iota((NB, NB), 0)
+    puts = []
+    for side in (0, 1):
+        alive = iota((NB, NB), 1) < live[0][:, side : side + 1]
+        gain = jnp.where(s == (0 if side == 0 else NSUB - 1), 0.0, -0.5)
+        puts.append(jnp.where((rows_i == recv[0, 0][side : side + 1, :]) & alive, gain, 0.0).astype(BF16))
     for copy in halo_send:
         copy.wait_recv()
     for side in (0, 1):
-        rows_i = iota((NB, NB), 0)
         took = jnp.where(rows_i == h_send[side][side : side + 1, :], 1.0, 0.0).astype(BF16)
-        alive = iota((NB, NB), 1) < live[0][:, side : side + 1]
-        puts = jnp.where((rows_i == recv[0, 0][side : side + 1, :]) & alive, 1.0, 0.0).astype(BF16)
-        both = lax.dot_general(took, puts, (((1,), (1,)), ((), ())), preferred_element_type=F32)
-        end = 0 if side == 0 else NSUB - 1
-        both = both * jnp.where(s == end, 0.0, -0.5)
+        both = lax.dot_general(took, puts[side], (((1,), (1,)), ((), ())), preferred_element_type=F32)
         link[NB * side : NB * side + NB, :] = both.astype(BF16)
 
     @pl.when(core == 0)
@@ -434,8 +435,11 @@
         row = jnp.where(lane == i, value, row)
     part3[4] = row
     plane3[core] = row
-    send_direct(0, 7)
-    send_plane3()
+    send_direct(0, 1)
+    send_plane3((31, 30, 29, 28, 27))
+    send_plane3(range(12, 27))
+    send_direct(1, 7)
+    send_plane3(reversed(range(12)))
     send_direct(7, len(DIRECT))
     g00 = h11 * h11 + h21 * h21
     inv00 = 1.0 / g00
@@ -463,8 +467,8 @@
     t1 = beta * h12 - factor * t0
     c1 = t1 / (g11 - factor * g01)
     c0 = (t0 - g01 * c1) * inv00
-    next_ref[0, 0] = (image - h12 * f_b1[...] - h22 * f_b2[...]) * (1.0 / h32)
-    sol_ref[0, 0] = guess[0, 0] + c0 * f_d1[...] + c1 * f_d2[...]
+    out_ref[1, 0, 0] = (image - h12 * f_b1[...] - h22 * f_b2[...]) * (1.0 / h32)
+    out_ref[0, 0, 0] = guess[0, 0] + c0 * f_d1[...] + c1 * f_d2[...]
 
     for copy in halo_guess + halo_send + halo_prolong + halo_e1 + halo_e2 + halo_sp1 + halo_sp2:
         copy.wait_send()
@@ -486,12 +490,11 @@
     hbm_spec = pl.BlockSpec(memory_space=pltpu.HBM)
     vmem_spec = pl.BlockSpec(memory_space=pltpu.VMEM)
     sides = (2, BS, NB)
-    shape = jax.ShapeDtypeStruct((1, 1, BS, NB), F32)
-    return pl.pallas_call(
+    both = pl.pallas_call(
         kernel,
-        out_shape=(shape, shape),
+        out_shape=jax.ShapeDtypeStruct((2, 1, 1, BS, NB), F32),
         in_specs=[hbm_spec] * 12,
-        out_specs=(vmem_spec, vmem_spec),
+        out_specs=vmem_spec,
         scratch_shapes=[
             *[pltpu.VMEM(args[i].shape, args[i].dtype) for i in (0, 1, 2, 3, 4, 5, 6, 7, 8, 10, 11)],
             pltpu.VMEM(sides, F32),
@@ -530,6 +533,7 @@
             collective_id=0, has_side_effects=True, vmem_limit_bytes=40 * 1024 * 1024
         ),
     )(*[pltpu.with_memory_space_constraint(a, pltpu.HBM) for a in args])
+    return both[0], both[1]
 
 
 def solution(mesh):

time: 68.4 us -> 67.8 us (level)
    unnamed x2 -> x0, local copies, waits for them, and re-layouts: 1.23 us -> none
where the time goes in v4:
time: 67.8 us; the launch traced here: 67.7 us
  Pallas kernels  66.4 us (98%)
    pallas_call x1, Pallas kernels, on_device(): pl.pallas_call(kernel, out_shape=jax.ShapeDtypeStruct((2, 1, 1, BS, NB),...  66.4 us

profile of v4, /device:TPU:1, one launch (start us, length us, event | category | flops | bytes accessed | tf_op | source)
XLA Modules:
  0.0 67.7 jit_solution(11956500196510569568)
XLA Ops:
  0.6 66.4 %shard_map.131 = f32[2,1,1,64,128]{4,3,2,1,0:T(8,128)S(1)} custom-call(f32[1,1,64,128]{3,2,1,0:T(8,128)} %rhs_h.1, f32[1,1,64,128]{3,2,1,0:T(8,128)} %guess_h.1, bf16[1,1,64,64,128]{4,3,2,1,0:T(8,128)(2,1)} %blocks_h.1, s32[1,1,128]{2,1,0:T(1,128)} %valve_h.1, f32[1,1,64,128]{3,2,1,0:T(8,128)} %jscale_h.1, f32[1,1,64,128]{3,2,1,0:T(8,128)} %prolong_h.1, ...), custom_call_target="tpu_custom_call" | custom-call | tf_op jit(solution)/shard_map/pallas_call | solution.py:493
  67.1 0.6 slice_bitcast_fusion
